TPU v7x, 32 devices: a whole 2x2x4 slice. The times are simulated.
32 devices in a mesh: dp: 8 (over y, x, core), seq: 4 (over z).
Axes of the slice: x: 2, y: 2, z: 4, core: 2. Of those that a mesh axis runs over, the one named last changes fastest.
Arguments:
- tokens: bfloat16 [8, 2048, 768], P('dp', 'seq'), may hold values from -6 to 6
- cotangent: bfloat16 [8, 2048, 768], P('dp', 'seq'), may hold values from -6 to 6
- segment_ids: int32 [8, 2048], P('dp', 'seq'), may hold values from 0 to 7, as said below
- doc_starts: int32 [8, 2048], P('dp', 'seq'), may hold values from 0 to 1, as said below
- valid_mask: int32 [8, 2048], P('dp', 'seq'), may hold values from 0 to 1
- step_number: int32 [1], replicated, may hold values from 1 to 64
- learn_rate: float32 [1], replicated, may hold values from 0.001 to 0.004
- norm_gain: float32 [768], replicated, may hold values from 0.5 to 1.5
- in_weight: bfloat16 [768, 3352], replicated, may hold values from -0.21875 to 0.21875
- conv_weight: float32 [4, 1792], replicated, may hold values from -3 to 3
- conv_bias: float32 [1792], replicated, may hold values from -1.75 to 1.75
- dt_bias: float32 [24], replicated, may hold values from -6 to -2
- a_log: float32 [24], replicated, may hold values from -1 to 2.5
- skip_d: float32 [24], replicated, may hold values from 0.5 to 1.5
- gate_gain: float32 [1536], replicated, may hold values from 0.5 to 1.5
- out_weight: bfloat16 [1536, 768], replicated, may hold values from -0.15625 to 0.15625
- in_momentum: float32 [768, 3352], P('seq'), may hold values from -6 to 6
- out_momentum: float32 [1536, 768], P(None, 'seq'), may hold values from -448 to 448
Outputs:
- output: bfloat16 [8, 2048, 768], P('dp', 'seq')
- input_grad: bfloat16 [8, 2048, 768], P('dp', 'seq')
- new_in_weight: bfloat16 [768, 3352], replicated
- new_out_weight: bfloat16 [1536, 768], replicated
- new_in_momentum: float32 [768, 3352], P('seq')
- new_out_momentum: float32 [1536, 768], P(None, 'seq')
- norm_gain_grad: float32 [768], replicated
- conv_weight_grad: float32 [4, 1792], replicated
- conv_bias_grad: float32 [1792], replicated
- dt_bias_grad: float32 [24], replicated
- a_log_grad: float32 [24], replicated
- skip_grad: float32 [24], replicated
- gate_gain_grad: float32 [1536], replicated
- output_rms: float32 [1], replicated
- mixer_rms: float32 [1], replicated
Inputs may be any that keep to these rules, and one draw needn't show every extreme that they name: Within each sequence segment_ids never fall, are 0 at the first position and rise by one exactly where doc_starts is 1; every sequence holds exactly 8 documents. `doc_starts`: 1 at the first position of every sequence; exactly 8 ones in every sequence.
All inputs are finite; a program needn't handle non-finite values.
Results may differ from a plain program's by a relative error of at most 0.0066.
The roundings to bfloat16 on the way count: a program that leaves them out, or rounds other values in their place, can miss the bound.
Values may be sent and summed in bfloat16 or wider, within the bound.
A program may use at most 192 MiB of HBM per device.

v0:
```python
import jax
import jax.numpy as jnp
from jax import lax
from jax.sharding import PartitionSpec as P

epsilon = 1e-05
highest = lax.Precision.HIGHEST


def shifted(block, axis, distance):
    devices = range(lax.axis_size(axis))
    route = [(i - distance, i) for i in devices if i - distance in devices]
    return lax.ppermute(block, axis, route)


def entering(value, axis, join, neutral):
    place = lax.axis_index(axis)
    gathered = jax.tree.map(
        lambda a, kind: lax.all_gather(a.astype(kind), axis), value, (jnp.bfloat16, jnp.bfloat16)
    )
    state = jax.tree.map(lambda a, e: jnp.zeros_like(a) + jnp.asarray(e, a.dtype), value, neutral)

    def one(step, state):
        return join(
            state,
            jax.tree.map(
                lambda a, own: lax.dynamic_index_in_dim(a, step, 0, False).astype(own.dtype),
                gathered,
                value,
            ),
        )

    return lax.fori_loop(0, place, one, state)


def carried_in(value, axis, combine, identity):
    length, mine = (lax.axis_size(axis), lax.axis_index(axis))
    everything = jax.tree.map(lambda part: lax.all_gather(part, axis), value)
    start = jax.tree.map(
        lambda part, zero: jnp.broadcast_to(jnp.asarray(zero, part.dtype), part.shape),
        value,
        identity,
    )

    def step(k, before):
        at = length - 1 - k
        reached = at > mine
        new = combine(before, jax.tree.map(lambda part: part[at], everything))
        return jax.tree.map(lambda a, b: jnp.where(reached, a, b), new, before)

    return lax.fori_loop(0, length, step, start)


def pre_norm(values, gain_values):
    return (
        values
        * lax.rsqrt(jnp.mean(values * values, axis=-1, keepdims=True) + epsilon)
        * gain_values
    )


def compose(earlier, later):
    return (earlier[0] * later[0], later[0][:, :, None, None] * earlier[1] + later[1])


def local(
    tokens,
    cotangent,
    segment_ids,
    doc_starts,
    valid_mask,
    step_number,
    learn_rate,
    norm_gain,
    in_weight,
    conv_weight,
    conv_bias,
    dt_bias,
    a_log,
    skip_d,
    gate_gain,
    out_weight,
    in_momentum,
    out_momentum,
):
    seq_count, piece_size, model_width = tokens.shape
    head_count = dt_bias.shape[0]
    tap_count, channels = conv_weight.shape
    inner_width = gate_gain.shape[0]
    state_width = (channels - inner_width) // 2
    head_width = inner_width // head_count
    proj_width = in_weight.shape[1]
    row_count = seq_count * piece_size
    inputs = tokens.astype(jnp.float32)
    normed_in, back_pre = jax.vjp(pre_norm, inputs, norm_gain)
    normed_low = normed_in.astype(jnp.bfloat16).reshape(row_count, model_width)
    projected = jnp.dot(normed_low, in_weight, preferred_element_type=jnp.float32).reshape(
        seq_count, piece_size, proj_width
    )
    gate_in = projected[:, :, :inner_width]
    conv_in = projected[:, :, inner_width : inner_width + channels]
    dt_raw = projected[:, :, inner_width + channels :]
    seg_float = segment_ids.astype(jnp.float32)
    prev_rows, prev_seg = shifted(
        (conv_in[:, piece_size - tap_count + 1 :], seg_float[:, piece_size - tap_count + 1 :]),
        "seq",
        1,
    )
    padded = jnp.concatenate([prev_rows, conv_in], axis=1)
    seg_pad = jnp.concatenate([prev_seg, seg_float], axis=1)
    masks = [
        (seg_pad[:, k : k + piece_size] == seg_float).astype(jnp.float32)[:, :, None]
        for k in range(tap_count)
    ]

    def conv_part(padded_in, taps_in, bias_in, raw_in, dt_bias_in, a_log_in):
        summed = bias_in + jnp.zeros((seq_count, piece_size, channels), jnp.float32)
        for k in range(tap_count):
            summed = summed + padded_in[:, k : k + piece_size] * masks[k] * taps_in[k]
        activated = jax.nn.silu(summed)
        signal = activated[:, :, :inner_width].reshape(
            seq_count, piece_size, head_count, head_width
        )
        writer = activated[:, :, inner_width : inner_width + state_width]
        reader = activated[:, :, inner_width + state_width :]
        step_size = jax.nn.softplus(raw_in + dt_bias_in)
        return (signal, writer, reader, step_size, -jnp.exp(a_log_in) * step_size)

    (signal, writer, reader, step_size, log_decay), back_conv = jax.vjp(
        conv_part, padded, conv_weight, conv_bias, dt_raw, dt_bias, a_log
    )
    counter = jnp.cumsum(doc_starts, axis=1)
    positions = jnp.arange(piece_size)
    causal = positions[:, None] >= positions[None, :]
    same_doc = (counter[:, :, None] == counter[:, None, :]) & causal[None]
    first_doc = (counter == 0)[:, :, None]
    last_doc = (counter == counter[:, -1:])[:, :, None]
    untouched = (counter[:, -1] == 0)[:, None]

    def end_state(signal_in, writer_in, step_in, decay_in):
        cumulative = jnp.cumsum(decay_in, axis=1)
        final_log = cumulative[:, -1]
        keeping = jnp.where(untouched, jnp.exp(final_log), 0.0)
        tails = jnp.where(last_doc, jnp.exp(final_log[:, None] - cumulative), 0.0) * step_in
        fresh_state = jnp.einsum(
            "slh,slhp,sln->shpn", tails, signal_in, writer_in, precision=highest
        )
        return (keeping, fresh_state)

    def piece_out(signal_in, writer_in, reader_in, step_in, decay_in, incoming_in):
        cumulative = jnp.cumsum(decay_in, axis=1)
        by_head = jnp.transpose(cumulative, (0, 2, 1))
        gaps = by_head[:, :, :, None] - by_head[:, :, None, :]
        decays = jnp.exp(jnp.where(same_doc[:, None], gaps, -1e30))
        scores = jnp.einsum("stn,sun->stu", reader_in, writer_in, precision=highest)
        weighted = scores[:, None] * decays
        inner_part = jnp.einsum(
            "shtu,suhp->sthp", weighted, signal_in * step_in[..., None], precision=highest
        )
        entries = jnp.where(first_doc, jnp.exp(cumulative), 0.0)
        carried = (
            jnp.einsum("stn,shpn->sthp", reader_in, incoming_in, precision=highest)
            * entries[..., None]
        )
        return inner_part + carried

    (keeping, fresh_state), back_end = jax.vjp(end_state, signal, writer, step_size, log_decay)
    identity = (jnp.ones_like(keeping), jnp.zeros_like(fresh_state))
    _, incoming = entering((keeping, fresh_state), "seq", compose, identity)
    ssm_out, back_out = jax.vjp(piece_out, signal, writer, reader, step_size, log_decay, incoming)

    def gate_norm(ssm_in, signal_in, skip_in, gate_values, gain_values):
        mixer_in = (ssm_in + skip_in[:, None] * signal_in).reshape(
            seq_count, piece_size, inner_width
        )
        gated_out = mixer_in * jax.nn.silu(gate_values)
        return (
            gated_out
            * lax.rsqrt(jnp.mean(gated_out * gated_out, axis=-1, keepdims=True) + epsilon)
            * gain_values
        )

    gate_normed, back_gate = jax.vjp(gate_norm, ssm_out, signal, skip_d, gate_in, gate_gain)
    gate_low = gate_normed.astype(jnp.bfloat16).reshape(row_count, inner_width)
    mixed = jnp.dot(gate_low, out_weight, preferred_element_type=jnp.float32).reshape(
        seq_count, piece_size, model_width
    )
    block_out = inputs + mixed
    valid_float = valid_mask.astype(jnp.float32)
    out_square = jnp.sum(valid_float * jnp.sum(block_out * block_out, axis=-1))
    mix_square = jnp.sum(valid_float * jnp.sum(mixed * mixed, axis=-1))
    valid_count = jnp.sum(valid_float)
    out_grad = cotangent.astype(jnp.float32) * valid_float[:, :, None]
    out_low = out_grad.astype(jnp.bfloat16).reshape(row_count, model_width)
    gate_grad = lax.dot_general(
        out_low, out_weight, (((1,), (1,)), ((), ())), preferred_element_type=jnp.float32
    ).reshape(seq_count, piece_size, inner_width)
    ssm_grad, signal_grad_gate, skip_grad, gate_in_grad, gate_gain_grad = back_gate(gate_grad)
    signal_grad_out, writer_grad_out, reader_grad, step_grad_out, decay_grad_out, state_grad = (
        back_out(ssm_grad)
    )
    _, later_grad = carried_in((keeping, state_grad), "seq", compose, identity)
    keeping_grad = jnp.sum(later_grad * incoming, axis=(2, 3))
    signal_grad_end, writer_grad_end, step_grad_end, decay_grad_end = back_end(
        (keeping_grad, later_grad)
    )
    padded_grad, conv_weight_grad, conv_bias_grad, dt_raw_grad, dt_bias_grad, a_log_grad = (
        back_conv(
            (
                signal_grad_gate + signal_grad_out + signal_grad_end,
                writer_grad_out + writer_grad_end,
                reader_grad,
                step_grad_out + step_grad_end,
                decay_grad_out + decay_grad_end,
            )
        )
    )
    rim_grad = shifted(padded_grad[:, : tap_count - 1].astype(jnp.bfloat16), "seq", -1).astype(
        jnp.float32
    )
    conv_in_grad = padded_grad[:, tap_count - 1 :] + jnp.pad(
        rim_grad, ((0, 0), (piece_size - tap_count + 1, 0), (0, 0))
    )
    proj_grad = (
        jnp.concatenate([gate_in_grad, conv_in_grad, dt_raw_grad], axis=2)
        .astype(jnp.bfloat16)
        .reshape(row_count, proj_width)
    )
    normed_grad = lax.dot_general(
        proj_grad, in_weight, (((1,), (1,)), ((), ())), preferred_element_type=jnp.float32
    ).reshape(seq_count, piece_size, model_width)
    input_grad_pre, norm_gain_grad = back_pre(normed_grad)
    input_grad = (out_grad + input_grad_pre).astype(jnp.bfloat16)
    share_rows = model_width // lax.axis_size("seq")
    in_part = lax.dot_general(
        normed_low, proj_grad, (((0,), (0,)), ((), ())), preferred_element_type=jnp.float32
    )
    out_part = lax.dot_general(
        out_low, gate_low, (((0,), (0,)), ((), ())), preferred_element_type=jnp.float32
    )
    whole_grad = lax.psum(jnp.concatenate([in_part, out_part], axis=1), "dp")
    grad_share = lax.psum_scatter(whole_grad, "seq", scatter_dimension=0, tiled=True)
    step_float = step_number[0].astype(jnp.float32)
    rate_now = learn_rate[0] * step_float / (step_float + 16.0)
    new_in_momentum = 0.5 * in_momentum + grad_share[:, :proj_width]
    new_out_momentum = 0.5 * out_momentum + jnp.transpose(grad_share[:, proj_width:])
    first_row = lax.axis_index("seq") * share_rows
    own_in = lax.dynamic_slice_in_dim(in_weight, first_row, share_rows, 0).astype(jnp.float32)
    own_out = lax.dynamic_slice_in_dim(out_weight, first_row, share_rows, 1).astype(jnp.float32)
    new_in_part = (own_in - rate_now * new_in_momentum).astype(jnp.bfloat16)
    new_out_part = (own_out - rate_now * new_out_momentum).astype(jnp.bfloat16)
    new_in_weight, new_out_weight = (
        lax.all_gather(new_in_part, "seq", axis=0, tiled=True),
        lax.all_gather(new_out_part, "seq", axis=1, tiled=True),
    )
    (
        norm_gain_total,
        conv_weight_total,
        conv_bias_total,
        dt_bias_total,
        a_log_total,
        skip_total,
        gate_gain_total,
        out_square_total,
        mix_square_total,
        valid_total,
    ) = lax.psum(
        (
            norm_gain_grad,
            conv_weight_grad,
            conv_bias_grad,
            dt_bias_grad,
            a_log_grad,
            skip_grad,
            gate_gain_grad,
            out_square,
            mix_square,
            valid_count,
        ),
        ("dp", "seq"),
    )
    denominator = jnp.maximum(valid_total, 1.0) * model_width
    output_rms = jnp.sqrt(out_square_total / denominator).reshape(1)
    mixer_rms = jnp.sqrt(mix_square_total / denominator).reshape(1)
    return (
        block_out.astype(jnp.bfloat16),
        input_grad,
        new_in_weight,
        new_out_weight,
        new_in_momentum,
        new_out_momentum,
        norm_gain_total,
        conv_weight_total,
        conv_bias_total,
        dt_bias_total,
        a_log_total,
        skip_total,
        gate_gain_total,
        output_rms,
        mixer_rms,
    )


def solution(mesh):
    placed = (
        P("dp", "seq", None),
        P("dp", "seq", None),
        P("dp", "seq"),
        P("dp", "seq"),
        P("dp", "seq"),
        P(),
        P(),
        P(),
        P(),
        P(),
        P(),
        P(),
        P(),
        P(),
        P(),
        P(),
        P("seq", None),
        P(None, "seq"),
    )
    return jax.shard_map(
        local,
        mesh=mesh,
        in_specs=placed,
        out_specs=(
            P("dp", "seq", None),
            P("dp", "seq", None),
            P(),
            P(),
            P("seq", None),
            P(None, "seq"),
            P(),
            P(),
            P(),
            P(),
            P(),
            P(),
            P(),
            P(),
            P(),
        ),
        check_vma=False,
    )
```

profile of v0, /device:TPU:0, one launch (start us, length us, event | category | flops | bytes accessed | tf_op | source)
XLA Modules:
  0.0 885.2 jit_solution(818629642145929513)
XLA Ops:
  9.2 5.5 convolution_bitcast_fusion
  14.8 4.9 collective-permute-start
  19.9 3.5 collective-permute-start.1
  25.9 4.2 slice.132
  36.3 11.6 %fusion.26 = (f32[1,512,1792]{2,1,0:T(8,128)S(1)}, f32[1,512,1792]{2,1,0:T(8,128)}) fusion(f32[1792]{0:T(1024)S(1)} %get-tuple-element.401, f32[1,512,1792]{2,1,0:T(8,128)} %slice.132, f32[512]{0:T(512)S(1)} %bitcast.377, f32[1792]{0:T(1024)S(1)} %get-tuple-element.402, f32[512]{0:T(512)S(1)} %bitcast.374, f32[1,3,1792]{2,1,0:T(4,128)S(1)} %copy.241, ...), kind=kLoop, calls=%fused_computation.50 | loop fusion | flops 17432576 | bytes 11075584 | tf_op jit(solution)/shard_map/jvp(jit(silu))/mul | solution.py:120
  54.3 4.3 fusion.70
  68.0 3.5 copy.254
  71.5 9.9 %all_gather.26 = bf16[4,1,24]{2,1,0:T(2,128)(2,1)} all-gather(bf16[1,1,24]{2,1,0:T(2,128)(2,1)} %get-tuple-element.453), channel_id=1, replica_groups=mesh['dp'=8,'seq'=4] {'seq'}, dimensions={0}, use_global_device_ids=true | all-gather | bytes 240 | tf_op jit(solution)/shard_map/all_gather | solution.py:19
  87.5 7.6 all-gather.11.cloned.1.call-done
  96.4 4.0 fusion.88
  100.5 29.3 %fusion.30 = f32[1,512,24,64]{1,3,2,0:T(8,128)} fusion(f32[1,512,24,64]{1,3,2,0:T(8,128)S(1)} %bitcast.337, f32[512,24,64]{0,2,1:T(8,128)S(1)} %fusion.88, f32[24]{0:T(128)S(1)} %copy-done.89, f32[512,24]{0,1:T(8,128)S(1)} %copy-done.35, f32[24,512]{1,0:T(8,128)S(1)} %copy-done.45, f32[512,512]{1,0:T(8,128)S(1)} %copy-done.27, ...), kind=kOutput, calls=%fused_computation.59 | convolution fusion | flops 4854644736 | bytes 14041184 | tf_op jit(solution)/shard_map/jvp(shtu,suhp->sthp)/dot_general | solution.py:157
  129.8 3.6 copy.252
  133.4 4.0 multiply_reduce_fusion.7
  141.5 5.6 multiply_reduce_fusion.5
  151.0 12.4 %copy.255 = f32[1,512,1536]{1,2,0:T(8,128)} copy(f32[1,512,1536]{2,1,0:T(8,128)} %mul.669) | data formatting | bytes 6291456 | tf_op jit(solution)/shard_map/transpose(jvp())/mul | solution.py:162
  163.4 5.4 fusion.107
  168.9 17.8 %all_gather.29 = f32[4,1,24]{2,1,0:T(1,128)} all-gather(f32[1,1,24]{2,1,0:T(1,128)S(1)} %copy-done.87), channel_id=1, replica_groups=mesh['dp'=8,'seq'=4] {'seq'}, dimensions={0}, use_global_device_ids=true | all-gather | bytes 480 | tf_op jit(solution)/shard_map/all_gather | solution.py:38
  186.7 3.5 copy.256
  190.2 3.7 multiply_reduce_fusion.6
  194.8 33.7 %fusion.7 = (f32[24,512]{1,0:T(8,128)}, f32[24,512]{1,0:T(8,128)S(1)}, f32[512,512]{1,0:T(8,128)}) fusion(f32[24,512]{1,0:T(8,128)} %bitcast_add_fusion.6, f32[512,512]{1,0:T(8,128)} %fusion.111, pred[512,512]{1,0:T(8,128)(4,1)} %fusion.81, f32[24,64,512]{2,1,0:T(8,128)} %bitcast.346, f32[512,24,64]{0,2,1:T(8,128)S(1)} %bitcast.339, f32[512,24]{0,1:T(8,128)} %copy.243), kind=kOutput, calls=%fused_computation.12 | convolution fusion | flops 4888961024 | bytes 8847360 | tf_op jit(solution)/shard_map/transpose(jvp(shtu,suhp->sthp))/dot_general | solution.py:157
  230.9 3.9 convolution_bitcast_fusion.1
  234.9 7.1 convolution_bitcast_fusion.2
  244.7 3.9 fusion.91
  248.6 22.4 %fusion.2 = f32[24,64,512]{2,1,0:T(8,128)} fusion(f32[24,64,512]{2,1,0:T(8,128)S(1)} %bitcast.347, f32[24,512]{1,0:T(8,128)S(1)} %copy-done.46, f32[512,512]{1,0:T(8,128)S(1)} %copy-done.28, pred[512,512]{1,0:T(8,128)(4,1)S(1)} %copy-done.33), kind=kOutput, calls=%fused_computation.9 | convolution fusion | flops 4850712576 | bytes 7651328 | tf_op jit(solution)/shard_map/transpose(jvp(shtu,suhp->sthp))/dot_general | solution.py:157
  271.0 12.0 %while.29 = (s32[]{:T(128)}, f32[1,24,64,128]{3,2,1,0:T(8,128)}, s32[]{:T(128)}, f32[4,1,24]{2,1,0:T(1,128)}, f32[4,1,24,64,128]{4,3,2,1,0:T(8,128)}, /*index=5*/s32[]{:T(128)}, s32[]{:T(128)}, s32[]{:T(128)}, s32[]{:T(128)}) while((s32[]{:T(128)}, f32[1,24,64,128]{3,2,1,0:T(8,128)}, s32[]{:T(128)}, f32[4,1,24]{2,1,0:T(1,128)}, ...), condition=%wide.region_11.12_spmd.clone, body=%wide.region_10.11_spmd.clone.sunk | while | flops 786440 | bytes 2359751 | solution.py:51
  283.0 4.1 fusion.34
  288.0 5.8 fusion.76
  293.8 4.2 fusion.33
  300.5 11.2 %multiply_reduce_fusion.3 = (f32[1792]{0:T(1024)}, f32[1792]{0:T(1024)S(1)}, f32[1792]{0:T(1024)}, f32[1792]{0:T(1024)S(1)}, f32[1792]{0:T(1024)}, /*index=5*/f32[1,512,1792]{2,1,0:T(8,128)S(1)}) fusion(f32[1,512,1792]{2,1,0:T(8,128)} %slice.132, f32[1,3,1792]{2,1,0:T(4,128)S(1)} %copy.241, f32[512]{0:T(512)S(1)} %bitcast.375, f32[512]{0:T(512)S(1)} %bitcast.369, ...), kind=kLoop, calls=%fused_computation.43 | loop fusion | flops 24763648 | bytes 18415616 | tf_op jit(solution)/shard_map/transpose(jvp())/reduce_sum | solution.py:119
  319.6 5.0 reduce-window.36
  324.8 5.0 reduce-window.34
  334.5 3.1 fusion.68
  337.7 5.8 pad_maximum_fusion
  343.4 15.2 %copy.289 = f32[768,4888]{1,0:T(8,128)} copy(f32[768,4888]{0,1:T(8,128)} %pad_maximum_fusion) | data formatting | bytes 30031872
  358.6 256.6 %reduce-scatter.4.cloned.1.call-done = f32[192,4888]{1,0:T(8,128)} async-done(((f32[768,4888]{1,0:T(8,128)}), f32[192,4888]{1,0:T(8,128)}) %reduce-scatter.4.cloned.1.call-update) | async-done | bytes 3754000
  615.2 5.7 copy.290
  622.9 89.6 %all-reduce.16.cloned.1.call-done = f32[192,4888]{0,1:T(8,128)} async-done(((f32[192,4888]{0,1:T(8,128)}), f32[192,4888]{0,1:T(8,128)}) %all-reduce.16.cloned.1.call-update) | async-done | bytes 3754000 | tf_op jit(solution)/shard_map/psum | solution.py:241
  712.5 3.5 subtract_convert_fusion.1
  717.1 3.6 copy.270
  720.7 6.4 subtract_convert_fusion
  727.1 3.8 copy.272
  731.3 3.3 multiply_reduce_fusion.8
  734.9 7.1 fusion.50
  742.6 42.8 %all-reduce.13 = (f32[768]{0:T(1024)}, f32[4,1792]{1,0:T(4,128)}, f32[1792]{0:T(1024)}, f32[24]{0:T(128)}, f32[24]{0:T(128)}, /*index=5*/f32[24]{0:T(128)}, f32[1536]{0:T(1024)}, f32[]{:T(128)}, f32[]{:T(128)}, f32[]{:T(128)}) all-reduce(f32[768]{0:T(1024)S(1)} %get-tuple-element.396, ...), channel_id=1, replica_groups=mesh['dp'=8,'seq'=4] {'dp','seq'}, use_global_device_ids=true, to_apply=%region_26.27 | all-reduce | flops 11339 | bytes 90712 | tf_op jit(solution)/shard_map/psum | solution.py:267
  787.5 3.3 fusion.52
  796.5 4.3 copy.276
  800.8 66.9 %all-gather.7.cloned.1.call-done = bf16[768,3352]{1,0:T(8,128)(2,1)} async-done(((bf16[192,3352]{1,0:T(8,128)(2,1)}), bf16[768,3352]{1,0:T(8,128)(2,1)}) %all-gather.7.cloned.1.call-update) | async-done | bytes 5148688 | tf_op jit(solution)/shard_map/all_gather | solution.py:253
  867.7 8.0 copy.275
  (306 shorter events, 82.4 us)
Async XLA Ops:
  7.2 88.0 %all-gather.11.cloned.1.call-start = ((), (), s32[]{:S(2)}) async-start(), calls=%async_computation.3 | async-start | bytes 1966080 | tf_op jit(solution)/shard_map/all_gather | solution.py:19
  9.2 5.6 copy-start.69
  9.2 10.6 %copy-start.72 = (s32[1,512]{1,0:T(1,128)S(1)}, s32[1,512]{1,0:T(1,128)}, u32[]{:S(2)}) copy-start(s32[1,512]{1,0:T(1,128)} %param.24) | copy-start | bytes 6148
  9.2 14.2 %copy-start.91 = (f32[24]{0:T(128)S(1)}, f32[24]{0:T(128)}, u32[]{:S(2)}) copy-start(f32[24]{0:T(128)} %param.34) | copy-start | bytes 292
  9.2 14.2 %copy-start.75 = (f32[24]{0:T(128)S(1)}, f32[24]{0:T(128)}, u32[]{:S(2)}) copy-start(f32[24]{0:T(128)} %param.33) | copy-start | bytes 292
  14.8 8.6 copy-start.4
  14.8 21.5 %collective-permute-start = (f32[1,3,1792]{2,0,1:T(1,128)S(1)}, f32[1,3,1792]{2,0,1:T(1,128)S(1)}, u32[]{:S(2)}, u32[]{:S(2)}) collective-permute-start(f32[1,3,1792]{2,0,1:T(1,128)S(1)} %copy.240), channel_id=1, source_target_pairs={{0,1},{1,2},{2,3},{4,5},{5,6},{6,7},{8,9},{9,10},{10,11},{12,13},{... | collective-permute-start | bytes 64520 | tf_op jit(solution)/shard_map/ppermute | solution.py:13
  19.9 16.3 %collective-permute-start.1 = (f32[1,3]{1,0:T(1,128)S(1)}, f32[1,3]{1,0:T(1,128)S(1)}, u32[]{:S(2)}, u32[]{:S(2)}) collective-permute-start(f32[1,3]{1,0:T(1,128)S(1)} %slice.135), channel_id=1, source_target_pairs={{0,1},{1,2},{2,3},{4,5},{5,6},{6,7},{8,9},{9,10},{10,11},{12,13},{... | collective-permute-start | bytes 44 | tf_op jit(solution)/shard_map/ppermute | solution.py:13
  25.8 10.2 %copy-start.63 = (f32[4,1792]{1,0:T(4,128)S(1)}, f32[4,1792]{1,0:T(4,128)}, u32[]{:S(2)}) copy-start(f32[4,1792]{1,0:T(4,128)} %param.31) | copy-start | bytes 86020
  25.8 10.5 %copy-start.74 = (f32[1792]{0:T(1024)S(1)}, f32[1792]{0:T(1024)}, u32[]{:S(2)}) copy-start(f32[1792]{0:T(1024)} %param.32) | copy-start | bytes 21508
  30.0 17.9 %copy-start.57 = (f32[1,512]{1,0:T(1,128)}, f32[1,512]{1,0:T(1,128)S(1)}, u32[]{:S(2)}) copy-start(f32[1,512]{1,0:T(1,128)S(1)} %compare_convert_fusion) | copy-start | bytes 6148
  30.8 17.1 %copy-start.62 = (s32[512]{0:T(512)}, s32[512]{0:T(512)S(1)}, u32[]{:S(2)}) copy-start(s32[512]{0:T(512)S(1)} %get-tuple-element.452) | copy-start | bytes 6148
  36.1 11.8 %copy-start.41 = (f32[1792]{0:T(1024)}, f32[1792]{0:T(1024)S(1)}, u32[]{:S(2)}) copy-start(f32[1792]{0:T(1024)S(1)} %get-tuple-element.401) | copy-start | bytes 21508
  36.2 11.8 %copy-start.43 = (f32[1792]{0:T(1024)}, f32[1792]{0:T(1024)S(1)}, u32[]{:S(2)}) copy-start(f32[1792]{0:T(1024)S(1)} %get-tuple-element.402) | copy-start | bytes 21508
  36.3 11.7 %copy-start.51 = (f32[1,512]{1,0:T(1,128)}, f32[1,512]{1,0:T(1,128)S(1)}, u32[]{:S(2)}) copy-start(f32[1,512]{1,0:T(1,128)S(1)} %get-tuple-element.470) | copy-start | bytes 6148
  36.3 11.7 %copy-start.53 = (f32[1,512]{1,0:T(1,128)}, f32[1,512]{1,0:T(1,128)S(1)}, u32[]{:S(2)}) copy-start(f32[1,512]{1,0:T(1,128)S(1)} %get-tuple-element.471) | copy-start | bytes 6148
  36.3 11.7 %copy-start.55 = (f32[1,512]{1,0:T(1,128)}, f32[1,512]{1,0:T(1,128)S(1)}, u32[]{:S(2)}) copy-start(f32[1,512]{1,0:T(1,128)S(1)} %get-tuple-element.472) | copy-start | bytes 6148
  58.7 212.3 %all-gather.13.cloned.1.call-start = ((), (), s32[]{:S(2)}) async-start(), calls=%async_computation.4 | async-start | bytes 3932160 | tf_op jit(solution)/shard_map/all_gather | solution.py:38
  100.4 29.4 %copy-start.14 = (f32[512,24,64]{0,2,1:T(8,128)}, f32[512,24,64]{0,2,1:T(8,128)S(1)}, u32[]{:S(2)}) copy-start(f32[512,24,64]{0,2,1:T(8,128)S(1)} %fusion.88) | copy-start | bytes 9437188
  141.5 7.3 copy-start.15
  163.4 5.5 copy-start.87
  168.8 446.4 %reduce-scatter.4.cloned.1.call-start = ((), (), s32[]{:S(2)}) async-start(), calls=%async_computation.6 | async-start | bytes 19169280
  230.9 11.1 %copy-start.18 = (f32[512,512]{1,0:T(8,128)S(1)}, f32[512,512]{1,0:T(8,128)}, u32[]{:S(2)}) copy-start(f32[512,512]{1,0:T(8,128)} %get-tuple-element.388) | copy-start | bytes 3145732
  230.9 13.7 %copy-start.7 = (f32[1,512,1536]{2,1,0:T(8,128)S(1)}, f32[1,512,1536]{2,1,0:T(8,128)}, u32[]{:S(2)}) copy-start(f32[1,512,1536]{2,1,0:T(8,128)} %copy-done.6) | copy-start | bytes 9437188
  230.9 13.7 %copy-start.17 = (bf16[1,512,768]{2,1,0:T(8,128)(2,1)S(1)}, bf16[1,512,768]{2,1,0:T(8,128)(2,1)}, u32[]{:S(2)}) copy-start(bf16[1,512,768]{2,1,0:T(8,128)(2,1)} %param.23) | copy-start | bytes 2359300
  230.9 13.7 %copy-start.48 = (f32[1536]{0:T(1024)S(1)}, f32[1536]{0:T(1024)}, u32[]{:S(2)}) copy-start(f32[1536]{0:T(1024)} %param.36) | copy-start | bytes 18436
  230.9 13.7 %copy-start.65 = (f32[512]{0:T(512)S(1)}, f32[512]{0:T(512)}, u32[]{:S(2)}) copy-start(f32[512]{0:T(512)} %copy-done.64) | copy-start | bytes 6148
  283.0 5.0 copy-start.29
  283.0 10.8 %copy-start.21 = (f32[24,64,512]{2,1,0:T(8,128)S(1)}, f32[24,64,512]{2,1,0:T(8,128)}, u32[]{:S(2)}) copy-start(f32[24,64,512]{2,1,0:T(8,128)} %fusion.2) | copy-start | bytes 9437188
  287.2 6.6 copy-start.11
  287.2 6.6 copy-start.37
  287.2 6.6 copy-start.90
  300.5 11.2 %copy-start.42 = (f32[1792]{0:T(1024)S(1)}, f32[1792]{0:T(1024)}, u32[]{:S(2)}) copy-start(f32[1792]{0:T(1024)} %copy-done.41) | copy-start | bytes 21508
  300.5 11.2 %copy-start.44 = (f32[1792]{0:T(1024)S(1)}, f32[1792]{0:T(1024)}, u32[]{:S(2)}) copy-start(f32[1792]{0:T(1024)} %copy-done.43) | copy-start | bytes 21508
  313.3 4.7 copy-start.30
  313.4 6.0 copy-start.86
  316.4 13.7 %copy-start.38 = (f32[512,24]{0,1:T(8,128)S(1)}, f32[512,24]{0,1:T(8,128)}, u32[]{:S(2)}) copy-start(f32[512,24]{0,1:T(8,128)} %get-tuple-element.466) | copy-start | bytes 147460
  316.4 13.9 %copy-start.85 = (f32[24]{0:T(128)S(1)}, f32[24]{0:T(128)}, u32[]{:S(2)}) copy-start(f32[24]{0:T(128)} %copy-done.84) | copy-start | bytes 292
  316.5 15.4 %collective-permute-start.2 = (bf16[1,3,1792]{2,1,0:T(4,128)(2,1)S(1)}, bf16[1,3,1792]{2,1,0:T(4,128)(2,1)S(1)}, u32[]{:S(2)}, u32[]{:S(2)}) collective-permute-start(bf16[1,3,1792]{2,1,0:T(4,128)(2,1)S(1)} %slice.284), channel_id=1, source_target_pairs={{1,0},{2,1},{3,2},{5,4},{6,5},{7,6},{9,8},{10,9},{11,10},{13,12},{... | collective-permute-start | bytes 32264 | tf_op jit(solution)/shard_map/ppermute | solution.py:13
  331.9 5.7 copy-start.39
  331.9 5.7 slice-start
  358.6 353.9 %all-reduce.16.cloned.1.call-start = ((), (), s32[]{:S(2)}) async-start(), calls=%async_computation.5 | async-start | bytes 10010624 | tf_op jit(solution)/shard_map/psum | solution.py:241
  621.0 175.6 %all-gather.9.cloned.1.call-start = ((), (), s32[]{:S(2)}) async-start(), calls=%async_computation.2 | async-start | bytes 2949120 | tf_op jit(solution)/shard_map/all_gather | solution.py:254
  717.1 150.7 %all-gather.7.cloned.1.call-start = ((), (), s32[]{:S(2)}) async-start(), calls=%async_computation.1 | async-start | bytes 6635520 | tf_op jit(solution)/shard_map/all_gather | solution.py:253
  734.8 7.2 copy-start.73
  734.8 7.8 copy-start.71
  734.9 52.6 %copy-start.68 = (f32[512]{0:T(512)S(1)}, f32[512]{0:T(512)}, u32[]{:S(2)}) copy-start(f32[512]{0:T(512)} %copy-done.67) | copy-start | bytes 6148
  742.0 48.8 %copy-start.13 = (f32[192,3352]{0,1:T(8,128)S(1)}, f32[192,3352]{0,1:T(8,128)}, u32[]{:S(2)}) copy-start(f32[192,3352]{0,1:T(8,128)} %get-tuple-element.444) | copy-start | bytes 7723012
  (56 other events, 191.2 us)
Sparse Core Ops, SparseCore 0:
  58.8 36.3 all-gather.10
  169.0 70.9 all-gather.12
  358.7 256.4 reduce-scatter.3
  621.1 91.3 all-reduce.15
  717.2 50.9 all-gather.8
  769.7 98.0 all-gather.6
where the time goes:
time: 895 us; the launch traced here: 885 us
  waiting for transfers between devices  421 us (47%)
  matrix products  151 us (17%)
  local copies, waits for them, and re-layouts  108 us (12%)
  other arithmetic  101 us (11%)
  blocking collectives  70.5 us (8%)
  between operations  23.1 us (3%)
  starting transfers between devices  10.1 us (1%)
    unnamed x7, waiting for transfers between devices  257 us
    psum x1, waiting for transfers between devices, local(): whole_grad = lax.psum(jnp.concatenate([in_part, out_part], axis=1), 'dp')  89.6 us
    dot_general x3, matrix products, piece_out(): jnp.einsum('shtu,suhp->sthp', weighted, signal_in * step_in[..., None], p...  85.3 us
    all_gather x1, waiting for transfers between devices, local(): lax.all_gather(new_in_part, 'seq', axis=0, tiled=True)  66.9 us
    unnamed x198, local copies, waits for them, and re-layouts  51 us
    psum x1, blocking collectives, local(): lax.psum((norm_gain_grad, conv_weight_grad, conv_bias_grad, dt_bias_grad,...  42.8 us
    mul x4, local copies, waits for them, and re-layouts, piece_out(): jnp.einsum('stn,shpn->sthp', reader_in, incoming_in, precision=highest)  20.4 us
  transfers between devices with their start and end apart: 9, of which 4 were waited for; matrix products, arithmetic and copies ran while one was open for 19% of the time, Pallas kernels for 0%

commit v1 on v0

--- a/solution.py
+++ b/solution.py
@@ -5,6 +5,28 @@
 
 epsilon = 1e-05
 highest = lax.Precision.HIGHEST
+
+
+def joined_along(blocks, dim):
+    shape = list(blocks.shape[1:])
+    shape[dim] *= blocks.shape[0]
+    return jnp.moveaxis(blocks, 0, dim).reshape(shape)
+
+
+def grow_blocks(x, axis):
+    length = lax.axis_size(axis)
+    tiles = x[None]
+    for level in range(length.bit_length() - 1):
+        bit = 1 << level
+        received = lax.ppermute(tiles, axis, [(i, i ^ bit) for i in range(length)])
+        both = jnp.stack([tiles, received])
+        upper = lax.axis_index(axis) >> level & 1
+        tiles = jnp.where(upper == 0, both, both[::-1]).reshape(-1, *x.shape)
+    return tiles
+
+
+def doubled_up(x, axis, dim):
+    return joined_along(grow_blocks(x, axis), dim)
 
 
 def shifted(block, axis, distance):
@@ -250,7 +272,7 @@
     new_in_part = (own_in - rate_now * new_in_momentum).astype(jnp.bfloat16)
     new_out_part = (own_out - rate_now * new_out_momentum).astype(jnp.bfloat16)
     new_in_weight, new_out_weight = (
-        lax.all_gather(new_in_part, "seq", axis=0, tiled=True),
+        doubled_up(new_in_part, "seq", 0),
         lax.all_gather(new_out_part, "seq", axis=1, tiled=True),
     )
     (

time: 895 us -> 987 us (1.10)
  blocking collectives: 70.5 us -> 148 us
  waiting for transfers between devices: 421 us -> 405 us
  local copies, waits for them, and re-layouts: 108 us -> 122 us
  other arithmetic: 101 us -> 113 us
    psum x1, blocking collectives: 42.8 us -> 120 us  [local(): lax.psum((norm_gain_grad, conv_weight_grad, conv_bias_grad, dt_bias_grad,...]
    all_gather x1 -> x0, waiting for transfers between devices: 66.9 us -> none  [local(): lax.all_gather(new_in_part, 'seq', axis=0, tiled=True)]
    ppermute x0 -> x2, waiting for transfers between devices: none -> 54 us  [grow_blocks(): received = lax.ppermute(tiles, axis, [(i, i ^ bit) for i in range(length)])]
    another operation x10 -> x13, other arithmetic: 14.3 us -> 21.8 us
    unnamed x7 -> x6, waiting for transfers between devices: 257 us -> 257 us
  transfers between devices with their start and end apart: 9 -> 10, of which waited for: 4 -> 4; matrix products, arithmetic and copies ran while one was open for 19% -> 18% of each run, Pallas kernels for 0% -> 0%
where the time goes in v1:
time: 987 us; the launch traced here: 976 us
  waiting for transfers between devices  405 us (41%)
  matrix products  151 us (15%)
  blocking collectives  148 us (15%)
  local copies, waits for them, and re-layouts  122 us (12%)
  other arithmetic  113 us (11%)
  between operations  22.5 us (2%)
  starting transfers between devices  13.7 us (1%)
    unnamed x6, waiting for transfers between devices  257 us
    psum x1, blocking collectives, local(): lax.psum((norm_gain_grad, conv_weight_grad, conv_bias_grad, dt_bias_grad,...  120 us
    psum x1, waiting for transfers between devices, local(): whole_grad = lax.psum(jnp.concatenate([in_part, out_part], axis=1), 'dp')  86.4 us
    dot_general x3, matrix products, piece_out(): jnp.einsum('shtu,suhp->sthp', weighted, signal_in * step_in[..., None], p...  85.3 us
    ppermute x2, waiting for transfers between devices, grow_blocks(): received = lax.ppermute(tiles, axis, [(i, i ^ bit) for i in range(length)])  54 us
    unnamed x198, local copies, waits for them, and re-layouts  52.2 us
  transfers between devices with their start and end apart: 10, of which 4 were waited for; matrix products, arithmetic and copies ran while one was open for 18% of the time, Pallas kernels for 0%

profile of v1, /device:TPU:0, one launch (start us, length us, event | category | flops | bytes accessed | tf_op | source)
XLA Modules:
  0.0 975.9 jit_solution(3664784382811690280)
XLA Ops:
  9.2 5.5 convolution_bitcast_fusion
  14.8 4.9 collective-permute-start
  19.9 3.5 collective-permute-start.1
  25.8 4.2 slice.132
  36.3 11.6 %fusion.26 = (f32[1,512,1792]{2,1,0:T(8,128)S(1)}, f32[1,512,1792]{2,1,0:T(8,128)}) fusion(f32[1792]{0:T(1024)S(1)} %get-tuple-element.401, f32[1,512,1792]{2,1,0:T(8,128)} %slice.132, f32[512]{0:T(512)S(1)} %bitcast.391, f32[1792]{0:T(1024)S(1)} %get-tuple-element.402, f32[512]{0:T(512)S(1)} %bitcast.388, f32[1,3,1792]{2,1,0:T(4,128)S(1)} %copy.259, ...), kind=kLoop, calls=%fused_computation.53 | loop fusion | flops 17432576 | bytes 11075584 | tf_op jit(solution)/shard_map/jvp(jit(silu))/mul | solution.py:142
  54.3 4.3 fusion.72
  68.0 3.5 copy.272
  71.5 9.9 %all_gather.23 = bf16[4,1,24]{2,1,0:T(2,128)(2,1)} all-gather(bf16[1,1,24]{2,1,0:T(2,128)(2,1)} %get-tuple-element.453), channel_id=1, replica_groups=mesh['dp'=8,'seq'=4] {'seq'}, dimensions={0}, use_global_device_ids=true | all-gather | bytes 240 | tf_op jit(solution)/shard_map/all_gather | solution.py:41
  87.5 7.6 all-gather.8.cloned.1.call-done
  96.6 4.0 fusion.90
  100.7 29.3 %fusion.30 = f32[1,512,24,64]{1,3,2,0:T(8,128)} fusion(f32[1,512,24,64]{1,3,2,0:T(8,128)S(1)} %bitcast.346, f32[512,24,64]{0,2,1:T(8,128)S(1)} %fusion.90, f32[24]{0:T(128)S(1)} %copy-done.89, f32[512,24]{0,1:T(8,128)S(1)} %copy-done.35, f32[24,512]{1,0:T(8,128)S(1)} %copy-done.45, f32[512,512]{1,0:T(8,128)S(1)} %copy-done.27, ...), kind=kOutput, calls=%fused_computation.63 | convolution fusion | flops 4854644736 | bytes 14041184 | tf_op jit(solution)/shard_map/jvp(shtu,suhp->sthp)/dot_general | solution.py:179
  130.0 3.6 copy.270
  133.5 4.0 multiply_reduce_fusion.7
  141.7 5.6 multiply_reduce_fusion.5
  151.2 3.7 copy.273
  154.9 5.4 fusion.109
  160.4 17.8 %all_gather.26 = f32[4,1,24]{2,1,0:T(1,128)} all-gather(f32[1,1,24]{2,1,0:T(1,128)S(1)} %copy-done.87), channel_id=1, replica_groups=mesh['dp'=8,'seq'=4] {'seq'}, dimensions={0}, use_global_device_ids=true | all-gather | bytes 480 | tf_op jit(solution)/shard_map/all_gather | solution.py:60
  178.2 3.5 copy.274
  181.8 3.7 multiply_reduce_fusion.6
  186.3 33.6 %fusion.7 = (f32[24,512]{1,0:T(8,128)}, f32[24,512]{1,0:T(8,128)S(1)}, f32[512,512]{1,0:T(8,128)}) fusion(f32[24,512]{1,0:T(8,128)} %bitcast_add_fusion.6, f32[512,512]{1,0:T(8,128)} %fusion.113, pred[512,512]{1,0:T(8,128)(4,1)} %fusion.83, f32[24,64,512]{2,1,0:T(8,128)} %bitcast.355, f32[512,24,64]{0,2,1:T(8,128)S(1)} %bitcast.348, f32[512,24]{0,1:T(8,128)} %copy.261), kind=kOutput, calls=%fused_computation.12 | convolution fusion | flops 4888961024 | bytes 8847360 | tf_op jit(solution)/shard_map/transpose(jvp(shtu,suhp->sthp))/dot_general | solution.py:179
  222.4 3.9 convolution_bitcast_fusion.1
  226.4 7.1 convolution_bitcast_fusion.2
  236.2 3.9 fusion.93
  240.1 22.4 %fusion.2 = f32[24,64,512]{2,1,0:T(8,128)} fusion(f32[24,64,512]{2,1,0:T(8,128)S(1)} %bitcast.356, f32[24,512]{1,0:T(8,128)S(1)} %copy-done.46, f32[512,512]{1,0:T(8,128)S(1)} %copy-done.28, pred[512,512]{1,0:T(8,128)(4,1)S(1)} %copy-done.33), kind=kOutput, calls=%fused_computation.9 | convolution fusion | flops 4850712576 | bytes 7651328 | tf_op jit(solution)/shard_map/transpose(jvp(shtu,suhp->sthp))/dot_general | solution.py:179
  262.5 12.0 %while.29 = (s32[]{:T(128)}, f32[1,24,64,128]{3,2,1,0:T(8,128)}, s32[]{:T(128)}, f32[4,1,24]{2,1,0:T(1,128)}, f32[4,1,24,64,128]{4,3,2,1,0:T(8,128)}, /*index=5*/s32[]{:T(128)}, s32[]{:T(128)}, s32[]{:T(128)}, s32[]{:T(128)}) while((s32[]{:T(128)}, f32[1,24,64,128]{3,2,1,0:T(8,128)}, s32[]{:T(128)}, f32[4,1,24]{2,1,0:T(1,128)}, ...), condition=%wide.region_11.12_spmd.clone, body=%wide.region_10.11_spmd.clone.sunk | while | flops 786440 | bytes 2359751 | solution.py:73
  274.6 4.1 fusion.34
  279.5 5.8 fusion.78
  285.4 4.2 fusion.33
  292.0 11.2 %multiply_reduce_fusion.3 = (f32[1792]{0:T(1024)}, f32[1792]{0:T(1024)S(1)}, f32[1792]{0:T(1024)}, f32[1792]{0:T(1024)S(1)}, f32[1792]{0:T(1024)}, /*index=5*/f32[1,512,1792]{2,1,0:T(8,128)S(1)}) fusion(f32[1,512,1792]{2,1,0:T(8,128)} %slice.132, f32[1,3,1792]{2,1,0:T(4,128)S(1)} %copy.259, f32[512]{0:T(512)S(1)} %bitcast.389, f32[512]{0:T(512)S(1)} %bitcast.383, ...), kind=kLoop, calls=%fused_computation.46 | loop fusion | flops 24763648 | bytes 18415616 | tf_op jit(solution)/shard_map/transpose(jvp())/reduce_sum | solution.py:141
  311.1 5.0 reduce-window.36
  316.3 5.0 reduce-window.34
  329.2 5.8 pad_maximum_fusion
  334.9 15.2 %copy.311 = f32[768,4888]{1,0:T(8,128)} copy(f32[768,4888]{0,1:T(8,128)} %pad_maximum_fusion) | data formatting | bytes 30031872
  350.1 256.6 %reduce-scatter.4.cloned.1.call-done = f32[192,4888]{1,0:T(8,128)} async-done(((f32[768,4888]{1,0:T(8,128)}), f32[192,4888]{1,0:T(8,128)}) %reduce-scatter.4.cloned.1.call-update) | async-done | bytes 3754000
  606.7 5.7 copy.312
  617.6 86.4 %all-reduce.16.cloned.1.call-done = f32[192,4888]{0,1:T(8,128)} async-done(((f32[192,4888]{0,1:T(8,128)}), f32[192,4888]{0,1:T(8,128)}) %all-reduce.16.cloned.1.call-update) | async-done | bytes 3754000 | tf_op jit(solution)/shard_map/psum | solution.py:263
  704.0 6.8 subtract_convert_fusion
  716.4 3.8 subtract_convert_fusion.1
  722.4 54.0 %collective-permute-done.3 = bf16[1,192,3352]{2,1,0:T(8,128)(2,1)} collective-permute-done((bf16[1,192,3352]{2,1,0:T(8,128)(2,1)}, bf16[1,192,3352]{2,1,0:T(8,128)(2,1)}, u32[]{:S(2)}, u32[]{:S(2)}) %collective-permute-start.3) | collective-permute-done | bytes 1287200 | tf_op jit(solution)/shard_map/ppermute | solution.py:21
  779.7 3.5 fusion.47
  783.3 5.6 copy.292
  794.9 7.1 fusion.52
  802.7 120.2 %all-reduce.13 = (f32[768]{0:T(1024)}, f32[4,1792]{1,0:T(4,128)}, f32[1792]{0:T(1024)}, f32[24]{0:T(128)}, f32[24]{0:T(128)}, /*index=5*/f32[24]{0:T(128)}, f32[1536]{0:T(1024)}, f32[]{:T(128)}, f32[]{:T(128)}, f32[]{:T(128)}) all-reduce(f32[768]{0:T(1024)S(1)} %get-tuple-element.396, ...), channel_id=1, replica_groups=mesh['dp'=8,'seq'=4] {'dp','seq'}, use_global_device_ids=true, to_apply=%region_26.27 | all-reduce | flops 11339 | bytes 90712 | tf_op jit(solution)/shard_map/psum | solution.py:289
  934.0 4.3 copy.298
  938.3 4.1 copy.293
  945.7 4.1 reverse_select_fusion
  949.8 9.1 copy.294
  958.9 8.0 copy.297
  (315 shorter events, 110.9 us)
Async XLA Ops:
  7.2 88.0 %all-gather.8.cloned.1.call-start = ((), (), s32[]{:S(2)}) async-start(), calls=%async_computation.2 | async-start | bytes 1966080 | tf_op jit(solution)/shard_map/all_gather | solution.py:41
  9.2 10.6 %copy-start.72 = (s32[1,512]{1,0:T(1,128)S(1)}, s32[1,512]{1,0:T(1,128)}, u32[]{:S(2)}) copy-start(s32[1,512]{1,0:T(1,128)} %param.24) | copy-start | bytes 6148
  9.2 14.2 %copy-start.91 = (f32[24]{0:T(128)S(1)}, f32[24]{0:T(128)}, u32[]{:S(2)}) copy-start(f32[24]{0:T(128)} %param.34) | copy-start | bytes 292
  9.2 14.2 %copy-start.75 = (f32[24]{0:T(128)S(1)}, f32[24]{0:T(128)}, u32[]{:S(2)}) copy-start(f32[24]{0:T(128)} %param.33) | copy-start | bytes 292
  14.8 8.6 copy-start.4
  14.8 21.5 %collective-permute-start = (f32[1,3,1792]{2,0,1:T(1,128)S(1)}, f32[1,3,1792]{2,0,1:T(1,128)S(1)}, u32[]{:S(2)}, u32[]{:S(2)}) collective-permute-start(f32[1,3,1792]{2,0,1:T(1,128)S(1)} %copy.258), channel_id=1, source_target_pairs={{0,1},{1,2},{2,3},{4,5},{5,6},{6,7},{8,9},{9,10},{10,11},{12,13},{... | collective-permute-start | bytes 64520 | tf_op jit(solution)/shard_map/ppermute | solution.py:35
  19.9 16.3 %collective-permute-start.1 = (f32[1,3]{1,0:T(1,128)S(1)}, f32[1,3]{1,0:T(1,128)S(1)}, u32[]{:S(2)}, u32[]{:S(2)}) collective-permute-start(f32[1,3]{1,0:T(1,128)S(1)} %slice.135), channel_id=1, source_target_pairs={{0,1},{1,2},{2,3},{4,5},{5,6},{6,7},{8,9},{9,10},{10,11},{12,13},{... | collective-permute-start | bytes 44 | tf_op jit(solution)/shard_map/ppermute | solution.py:35
  25.8 10.2 %copy-start.63 = (f32[4,1792]{1,0:T(4,128)S(1)}, f32[4,1792]{1,0:T(4,128)}, u32[]{:S(2)}) copy-start(f32[4,1792]{1,0:T(4,128)} %param.31) | copy-start | bytes 86020
  25.8 10.5 %copy-start.74 = (f32[1792]{0:T(1024)S(1)}, f32[1792]{0:T(1024)}, u32[]{:S(2)}) copy-start(f32[1792]{0:T(1024)} %param.32) | copy-start | bytes 21508
  30.0 17.9 %copy-start.57 = (f32[1,512]{1,0:T(1,128)}, f32[1,512]{1,0:T(1,128)S(1)}, u32[]{:S(2)}) copy-start(f32[1,512]{1,0:T(1,128)S(1)} %compare_convert_fusion) | copy-start | bytes 6148
  30.8 17.1 %copy-start.62 = (s32[512]{0:T(512)}, s32[512]{0:T(512)S(1)}, u32[]{:S(2)}) copy-start(s32[512]{0:T(512)S(1)} %get-tuple-element.452) | copy-start | bytes 6148
  36.1 11.8 %copy-start.41 = (f32[1792]{0:T(1024)}, f32[1792]{0:T(1024)S(1)}, u32[]{:S(2)}) copy-start(f32[1792]{0:T(1024)S(1)} %get-tuple-element.401) | copy-start | bytes 21508
  36.1 11.8 %copy-start.43 = (f32[1792]{0:T(1024)}, f32[1792]{0:T(1024)S(1)}, u32[]{:S(2)}) copy-start(f32[1792]{0:T(1024)S(1)} %get-tuple-element.402) | copy-start | bytes 21508
  36.3 11.7 %copy-start.51 = (f32[1,512]{1,0:T(1,128)}, f32[1,512]{1,0:T(1,128)S(1)}, u32[]{:S(2)}) copy-start(f32[1,512]{1,0:T(1,128)S(1)} %get-tuple-element.472) | copy-start | bytes 6148
  36.3 11.7 %copy-start.53 = (f32[1,512]{1,0:T(1,128)}, f32[1,512]{1,0:T(1,128)S(1)}, u32[]{:S(2)}) copy-start(f32[1,512]{1,0:T(1,128)S(1)} %get-tuple-element.473) | copy-start | bytes 6148
  36.3 11.7 %copy-start.55 = (f32[1,512]{1,0:T(1,128)}, f32[1,512]{1,0:T(1,128)S(1)}, u32[]{:S(2)}) copy-start(f32[1,512]{1,0:T(1,128)S(1)} %get-tuple-element.474) | copy-start | bytes 6148
  58.6 203.8 %all-gather.10.cloned.1.call-start = ((), (), s32[]{:S(2)}) async-start(), calls=%async_computation.3 | async-start | bytes 3932160 | tf_op jit(solution)/shard_map/all_gather | solution.py:60
  100.6 29.4 %copy-start.14 = (f32[512,24,64]{0,2,1:T(8,128)}, f32[512,24,64]{0,2,1:T(8,128)S(1)}, u32[]{:S(2)}) copy-start(f32[512,24,64]{0,2,1:T(8,128)S(1)} %fusion.90) | copy-start | bytes 9437188
  141.7 7.3 copy-start.15
  160.3 446.4 %reduce-scatter.4.cloned.1.call-start = ((), (), s32[]{:S(2)}) async-start(), calls=%async_computation.5 | async-start | bytes 19169280
  222.4 11.1 %copy-start.18 = (f32[512,512]{1,0:T(8,128)S(1)}, f32[512,512]{1,0:T(8,128)}, u32[]{:S(2)}) copy-start(f32[512,512]{1,0:T(8,128)} %get-tuple-element.388) | copy-start | bytes 3145732
  222.4 13.7 %copy-start.7 = (f32[1,512,1536]{2,1,0:T(8,128)S(1)}, f32[1,512,1536]{2,1,0:T(8,128)}, u32[]{:S(2)}) copy-start(f32[1,512,1536]{2,1,0:T(8,128)} %copy-done.6) | copy-start | bytes 9437188
  222.4 13.7 %copy-start.17 = (bf16[1,512,768]{2,1,0:T(8,128)(2,1)S(1)}, bf16[1,512,768]{2,1,0:T(8,128)(2,1)}, u32[]{:S(2)}) copy-start(bf16[1,512,768]{2,1,0:T(8,128)(2,1)} %param.23) | copy-start | bytes 2359300
  222.4 13.7 %copy-start.48 = (f32[1536]{0:T(1024)S(1)}, f32[1536]{0:T(1024)}, u32[]{:S(2)}) copy-start(f32[1536]{0:T(1024)} %param.36) | copy-start | bytes 18436
  222.4 13.7 %copy-start.65 = (f32[512]{0:T(512)S(1)}, f32[512]{0:T(512)}, u32[]{:S(2)}) copy-start(f32[512]{0:T(512)} %copy-done.64) | copy-start | bytes 6148
  274.5 10.8 %copy-start.21 = (f32[24,64,512]{2,1,0:T(8,128)S(1)}, f32[24,64,512]{2,1,0:T(8,128)}, u32[]{:S(2)}) copy-start(f32[24,64,512]{2,1,0:T(8,128)} %fusion.2) | copy-start | bytes 9437188
  278.7 6.6 copy-start.11
  278.7 6.6 copy-start.37
  278.7 6.6 copy-start.90
  292.0 11.2 %copy-start.42 = (f32[1792]{0:T(1024)S(1)}, f32[1792]{0:T(1024)}, u32[]{:S(2)}) copy-start(f32[1792]{0:T(1024)} %copy-done.41) | copy-start | bytes 21508
  292.0 11.2 %copy-start.44 = (f32[1792]{0:T(1024)S(1)}, f32[1792]{0:T(1024)}, u32[]{:S(2)}) copy-start(f32[1792]{0:T(1024)} %copy-done.43) | copy-start | bytes 21508
  304.9 6.0 copy-start.86
  307.9 13.7 %copy-start.38 = (f32[512,24]{0,1:T(8,128)S(1)}, f32[512,24]{0,1:T(8,128)}, u32[]{:S(2)}) copy-start(f32[512,24]{0,1:T(8,128)} %get-tuple-element.468) | copy-start | bytes 147460
  307.9 13.9 %copy-start.85 = (f32[24]{0:T(128)S(1)}, f32[24]{0:T(128)}, u32[]{:S(2)}) copy-start(f32[24]{0:T(128)} %copy-done.84) | copy-start | bytes 292
  308.0 15.4 %collective-permute-start.2 = (bf16[1,3,1792]{2,1,0:T(4,128)(2,1)S(1)}, bf16[1,3,1792]{2,1,0:T(4,128)(2,1)S(1)}, u32[]{:S(2)}, u32[]{:S(2)}) collective-permute-start(bf16[1,3,1792]{2,1,0:T(4,128)(2,1)S(1)} %slice.284), channel_id=1, source_target_pairs={{1,0},{2,1},{3,2},{5,4},{6,5},{7,6},{9,8},{10,9},{11,10},{13,12},{... | collective-permute-start | bytes 32264 | tf_op jit(solution)/shard_map/ppermute | solution.py:35
  323.4 5.7 slice-start
  350.1 353.9 %all-reduce.16.cloned.1.call-start = ((), (), s32[]{:S(2)}) async-start(), calls=%async_computation.4 | async-start | bytes 10010624 | tf_op jit(solution)/shard_map/psum | solution.py:263
  612.5 321.5 %all-gather.6.cloned.1.call-start = ((), (), s32[]{:S(2)}) async-start(), calls=%async_computation.1 | async-start | bytes 2949120 | tf_op jit(solution)/shard_map/all_gather | solution.py:276
  713.2 63.2 %collective-permute-start.3 = (bf16[1,192,3352]{2,1,0:T(8,128)(2,1)}, bf16[1,192,3352]{2,1,0:T(8,128)(2,1)}, u32[]{:S(2)}, u32[]{:S(2)}) collective-permute-start(bf16[1,192,3352]{2,1,0:T(8,128)(2,1)} %copy.290), channel_id=1, source_target_pairs={{0,1},{1,0},{2,3},{3,2},{4,5},{5,4},{6,7},{7,6},{8,9},{9,8},{10,11... | collective-permute-start | bytes 3861512 | tf_op jit(solution)/shard_map/ppermute | solution.py:21
  783.3 7.8 copy-start.50
  783.3 8.0 copy-start.8
  783.3 8.0 copy-start.49
  783.3 8.0 copy-start.66
  788.9 149.4 %collective-permute-start.4 = (bf16[2,192,3352]{2,1,0:T(8,128)(2,1)}, bf16[2,192,3352]{2,1,0:T(8,128)(2,1)}, u32[]{:S(2)}, u32[]{:S(2)}) collective-permute-start(bf16[2,192,3352]{2,1,0:T(8,128)(2,1)} %copy.292), channel_id=1, source_target_pairs={{0,2},{1,3},{2,0},{3,1},{4,6},{5,7},{6,4},{7,5},{8,10},{9,11},{10,... | collective-permute-start | bytes 7723016 | tf_op jit(solution)/shard_map/ppermute | solution.py:21
  794.9 7.2 copy-start.73
  794.9 7.8 copy-start.71
  794.9 130.0 %copy-start.68 = (f32[512]{0:T(512)S(1)}, f32[512]{0:T(512)}, u32[]{:S(2)}) copy-start(f32[512]{0:T(512)} %copy-done.67) | copy-start | bytes 6148
  802.0 126.2 %copy-start.13 = (f32[192,3352]{0,1:T(8,128)S(1)}, f32[192,3352]{0,1:T(8,128)}, u32[]{:S(2)}) copy-start(f32[192,3352]{0,1:T(8,128)} %get-tuple-element.444) | copy-start | bytes 7723012
  (57 other events, 201.9 us)
Sparse Core Ops, SparseCore 0:
  58.8 36.3 all-gather.7
  160.4 70.9 all-gather.9
  350.2 256.4 reduce-scatter.3
  612.6 91.3 all-reduce.15
  722.5 60.0 all-gather.5
